TPU v7x, 256 devices: a whole 4x4x8 slice. The times are simulated.
256 devices in a mesh: seq: 64 (over z, y, core), tp: 4 (over x).
Axes of the slice: x: 4, y: 4, z: 8, core: 2. Of those that a mesh axis runs over, the one named last changes fastest.
Arguments:
- hidden_in: bfloat16 [1536, 8192], P('seq', 'tp'), may hold values from -8 to 8
- kv_weight: bfloat16 [8192, 1024], P('tp'), may hold values from -0.0625 to 0.0625
- queries: bfloat16 [1536, 4096], P('seq', 'tp'), may hold values from -15 to 15
- prefix_keys: bfloat16 [512, 128, 512], P('seq', None, 'tp'), may hold values from -6 to 6
- prefix_values: bfloat16 [512, 128, 512], P('seq', None, 'tp'), may hold values from -6 to 6
- page_table: int32 [512], replicated, may hold values from 0 to 511, each once
- suffix_lengths: int32 [2, 8], replicated, may hold values from 1 to 160, 768 in all within a row
- out_weight: bfloat16 [4096, 4096], P('tp'), may hold values from -0.09375 to 0.09375
Outputs:
- hidden: bfloat16 [1536, 4096], P('seq', 'tp')
- new_pages: bfloat16 [1536, 1024], P('seq', 'tp')
Inputs may be any that keep to these rules, and one draw needn't show every extreme that they name: `page_table`: a permutation of the 512 cache pages; entries 256 * g to 256 * g + 255 are group g's prefix pages. `suffix_lengths`: each row sums to 768; group g's requests take its suffix tokens in order of their place u; some request has exactly 160 tokens.
All inputs are finite; a program needn't handle non-finite values.
Results may differ from a plain program's by a relative error of at most 0.0095.
Values may be sent and summed in bfloat16 or wider, within the bound.
A program may use at most 192 MiB of HBM per device.

v0:
```python
import math

import jax
import jax.numpy as jnp
from jax import lax
from jax.sharding import PartitionSpec as P

HD = 128
PAGE = 128
GROUPS = 2
REQS = 8
LONGEST = 160


masked_score = -1e30


def in_blocks(array, dim, length):
    before, after = (array.shape[:dim], array.shape[dim + 1 :])
    return jnp.moveaxis(array.reshape(*before, length, -1, *after), dim, 0)


def sent_and_summed(array, axis, dim):
    parts = in_blocks(array, dim, lax.axis_size(axis))
    arrived = lax.all_to_all(parts, axis, split_axis=0, concat_axis=0, tiled=True)
    return arrived.sum(axis=0)


def sent_together(arrays, axis, dim, along):
    both = jnp.concatenate(arrays, axis=along)
    result, at, gathered = (lax.all_gather(both, axis, axis=dim, tiled=True), 0, [])
    for a in arrays:
        gathered.append(lax.slice_in_dim(result, at, at + a.shape[along], axis=along))
        at += a.shape[along]
    return tuple(gathered)


def passed_along(array, axis, by):
    length = lax.axis_size(axis)
    pairs = [(i, i + by) for i in range(length) if 0 <= i + by < length]
    return lax.ppermute(array, axis, pairs)


def place_tokens(tokens, block_rows):
    blocks = tokens // block_rows
    groups = blocks % GROUPS
    within = blocks // GROUPS * block_rows + tokens % block_rows
    return (groups, within)


def token_table(groups, within, lengths):
    picker = (groups[:, None] == jnp.arange(GROUPS, dtype=jnp.int32)[None, :]).astype(jnp.int32)
    end_marks = jnp.cumsum(lengths, axis=1)
    token_ends = jnp.sum(picker[:, :, None] * end_marks[None, :, :], axis=1)
    token_lens = jnp.sum(picker[:, :, None] * lengths[None, :, :], axis=1)
    passed = (within[:, None] >= token_ends).astype(jnp.int32)
    request = jnp.sum(passed, axis=1)
    offset = within - jnp.sum(passed * token_lens, axis=1)
    return (groups * REQS + request, offset)


def rotate(key_rows, positions):
    half_dim = HD // 2
    frequency = jnp.power(500000.0, -(jnp.arange(half_dim, dtype=jnp.float32) * 2.0 / HD))
    angles = positions.astype(jnp.float32)[:, None] * frequency[None, :]
    cosine = jnp.cos(angles)[:, None, :]
    sine_part = jnp.sin(angles)[:, None, :]
    leading = key_rows[..., :half_dim]
    trailing = key_rows[..., half_dim:]
    return jnp.concatenate(
        [leading * cosine - trailing * sine_part, trailing * cosine + leading * sine_part], axis=-1
    )


def slot_groups(slot_ids, page_table, group_pages):
    matches = page_table[None, :] == slot_ids[:, None]
    owners = jnp.arange(page_table.shape[0], dtype=jnp.int32) // group_pages
    return jnp.sum(jnp.where(matches, owners[None, :], 0), axis=1)


def online_update(running, scores, usable, values):
    row_top, totals, mixed_sum = running
    kept_scores = jnp.where(usable, scores, masked_score)
    new_top = jnp.maximum(row_top, jnp.max(kept_scores, axis=-1))
    weights = jnp.exp(kept_scores - new_top[..., None]) * usable.astype(jnp.float32)
    factor = jnp.exp(row_top - new_top)
    totals = totals * factor + jnp.sum(weights, axis=-1)
    product = jnp.einsum(
        "tkgp,pkd->tkgd", weights.astype(jnp.bfloat16), values, preferred_element_type=jnp.float32
    )
    mixed_sum = mixed_sum * factor[..., None] + product
    return (new_top, totals, mixed_sum)


def blank_state(row_count, kv_heads, group_q):
    return (
        jnp.full((row_count, kv_heads, group_q), masked_score, jnp.float32),
        jnp.zeros((row_count, kv_heads, group_q), jnp.float32),
        jnp.zeros((row_count, kv_heads, group_q, HD), jnp.float32),
    )


def local(
    hidden_in,
    kv_weight,
    queries,
    prefix_keys,
    prefix_values,
    page_table,
    suffix_lengths,
    out_weight,
):
    row_count = hidden_in.shape[0]
    seq_count = lax.axis_size("seq")
    seq_rank = lax.axis_index("seq")
    suffix_total = row_count * seq_count
    half_total = suffix_total // GROUPS
    pages_here = prefix_keys.shape[0]
    group_pages = pages_here * seq_count // GROUPS
    prefix_len = group_pages * PAGE
    kv_heads = prefix_keys.shape[2] // HD
    head_count = queries.shape[1] // HD
    group_q = head_count // kv_heads
    score_scale = 1.0 / math.sqrt(HD)
    partial_kv = jnp.dot(hidden_in, kv_weight, preferred_element_type=jnp.float32)
    local_kv = sent_and_summed(partial_kv, "tp", 1).reshape(row_count, kv_heads, 2, HD)
    tokens = seq_rank * row_count + jnp.arange(row_count, dtype=jnp.int32)
    groups, within = place_tokens(tokens, row_count)
    request_ids, offsets = token_table(groups, within, suffix_lengths)
    rotated = rotate(local_kv[:, :, 0], prefix_len + offsets)
    new_pages = (
        jnp.stack([rotated, local_kv[:, :, 1]], axis=2)
        .reshape(row_count, kv_heads * 2 * HD)
        .astype(jnp.bfloat16)
    )
    query_block = queries.reshape(row_count, kv_heads, group_q, HD)
    my_group = seq_rank % GROUPS
    my_block = seq_rank // GROUPS
    piece_keys, piece_vals = sent_together((prefix_keys, prefix_values), "seq", 0, 1)
    piece_count = piece_keys.shape[0]
    turn_pages = math.gcd(piece_count, 8)

    def one_turn(turn_index, running):
        offset_row = turn_index * turn_pages
        keys_now = lax.dynamic_slice_in_dim(piece_keys, offset_row, turn_pages, 0).reshape(
            turn_pages * PAGE, kv_heads, HD
        )
        vals_now = lax.dynamic_slice_in_dim(piece_vals, offset_row, turn_pages, 0).reshape(
            turn_pages * PAGE, kv_heads, HD
        )
        slot_ids = offset_row + jnp.arange(turn_pages, dtype=jnp.int32)
        usable = jnp.repeat(slot_groups(slot_ids, page_table, group_pages) == my_group, PAGE)
        scores = (
            jnp.einsum("tkgd,pkd->tkgp", query_block, keys_now, preferred_element_type=jnp.float32)
            * score_scale
        )
        return online_update(running, scores, usable[None, None, None, :], vals_now)

    prefix_state = lax.fori_loop(
        0, piece_count // turn_pages, one_turn, blank_state(row_count, kv_heads, group_q)
    )
    reach_blocks = (min(LONGEST, half_total - REQS + 1) + row_count - 2) // row_count
    earlier = []
    for distance in range(reach_blocks, 0, -1):
        earlier.append(passed_along(new_pages, "seq", GROUPS * distance))
    window = jnp.concatenate(earlier + [new_pages], axis=0)
    window_len = window.shape[0]
    window_places = (my_block - reach_blocks) * row_count + jnp.arange(window_len, dtype=jnp.int32)
    inside = window_places >= 0
    window_groups = jnp.zeros((window_len,), jnp.int32) + my_group
    window_ids, unused_offsets = token_table(
        window_groups, jnp.maximum(window_places, 0), suffix_lengths
    )
    visible = (
        inside[None, :]
        & (window_ids[None, :] == request_ids[:, None])
        & (window_places[None, :] <= within[:, None])
    )
    window_kv = window.reshape(window_len, kv_heads, 2, HD)
    suffix_scores = (
        jnp.einsum(
            "tkgd,pkd->tkgp", query_block, window_kv[:, :, 0], preferred_element_type=jnp.float32
        )
        * score_scale
    )
    final_top, totals, mixed_sum = online_update(
        prefix_state, suffix_scores, visible[:, None, None, :], window_kv[:, :, 1]
    )
    attended = (
        (mixed_sum / totals[..., None]).reshape(row_count, head_count * HD).astype(jnp.bfloat16)
    )
    partial_out = jnp.dot(attended, out_weight, preferred_element_type=jnp.float32)
    hidden = sent_and_summed(partial_out, "tp", 1).astype(jnp.bfloat16)
    return (hidden, new_pages)


def solution(mesh):
    return jax.shard_map(
        local,
        mesh=mesh,
        in_specs=(
            P("seq", "tp"),
            P("tp", None),
            P("seq", "tp"),
            P("seq", None, "tp"),
            P("seq", None, "tp"),
            P(),
            P(),
            P("tp", None),
        ),
        out_specs=(P("seq", "tp"), P("seq", "tp")),
        check_vma=False,
    )
```

profile of v0, /device:TPU:1, one launch (start us, length us, event | category | flops | bytes accessed | tf_op | source)
XLA Modules:
  0.0 363.7 jit_solution(9231079365247932364)
XLA Ops:
  7.2 1.9 pad_maximum_fusion
  9.1 2.8 fusion.48
  12.6 4.8 %all-to-all-start = ((f32[4,24,256]{2,1,0:T(8,128)}), f32[4,24,256]{2,1,0:T(8,128)S(1)}, u32[]{:S(2)}, u32[]{:S(2)}) async-start(f32[4,24,256]{2,1,0:T(8,128)} %bitcast.133), calls=%async_computation | async-start | bytes 196608 | tf_op jit(solution)/shard_map/all_to_all | solution.py:25
  19.3 2.8 all-to-all-done
  22.5 6.0 %collective-permute-start = (bf16[24,256]{1,0:T(8,128)(2,1)S(1)}, bf16[24,256]{1,0:T(8,128)(2,1)S(1)}, u32[]{:S(2)}, u32[]{:S(2)}) collective-permute-start(bf16[24,256]{1,0:T(8,128)(2,1)S(1)} %bitcast.169), channel_id=1, source_target_pairs={{0,56},{4,60},{8,64},{12,68},{16,72},{20,76},{24,80},{28,84},{32,8... | collective-permute-start | bytes 36872 | tf_op jit(solution)/shard_map/ppermute | solution.py:41
  29.4 12.0 %copy.36 = bf16[4096,1024]{1,0:T(8,128)(2,1)} copy(bf16[4096,1024]{0,1:T(8,128)(2,1)} %bitcast.160) | data formatting | bytes 16777216 | tf_op jit(solution)/shard_map/dot_general | solution.py:192
  41.4 4.9 %collective-permute-start.1 = (bf16[24,256]{1,0:T(8,128)(2,1)S(1)}, bf16[24,256]{1,0:T(8,128)(2,1)S(1)}, u32[]{:S(2)}, u32[]{:S(2)}) collective-permute-start(bf16[24,256]{1,0:T(8,128)(2,1)S(1)} %bitcast.170), channel_id=1, source_target_pairs={{0,48},{4,52},{8,56},{12,60},{16,64},{20,68},{24,72},{28,76},{32,8... | collective-permute-start | bytes 36872 | tf_op jit(solution)/shard_map/ppermute | solution.py:41
  46.4 5.2 %collective-permute-start.2 = (bf16[24,256]{1,0:T(8,128)(2,1)S(1)}, bf16[24,256]{1,0:T(8,128)(2,1)S(1)}, u32[]{:S(2)}, u32[]{:S(2)}) collective-permute-start(bf16[24,256]{1,0:T(8,128)(2,1)S(1)} %bitcast.171), channel_id=1, source_target_pairs={{0,40},{4,44},{8,48},{12,52},{16,56},{20,60},{24,64},{28,68},{32,7... | collective-permute-start | bytes 36872 | tf_op jit(solution)/shard_map/ppermute | solution.py:41
  51.6 2.7 collective-permute-start.3
  54.2 4.4 %collective-permute-start.4 = (bf16[24,256]{1,0:T(8,128)(2,1)S(1)}, bf16[24,256]{1,0:T(8,128)(2,1)S(1)}, u32[]{:S(2)}, u32[]{:S(2)}) collective-permute-start(bf16[24,256]{1,0:T(8,128)(2,1)S(1)} %bitcast.173), channel_id=1, source_target_pairs={{0,24},{4,28},{8,32},{12,36},{16,40},{20,44},{24,48},{28,52},{32,5... | collective-permute-start | bytes 36872 | tf_op jit(solution)/shard_map/ppermute | solution.py:41
  58.7 3.2 collective-permute-start.5
  61.9 1.3 collective-permute-start.6
  64.6 92.2 %all-gather.2.cloned.1.call-done = bf16[512,256,128]{2,1,0:T(8,128)(2,1)} async-done(((bf16[8,256,128]{2,1,0:T(8,128)(2,1)}), bf16[512,256,128]{2,1,0:T(8,128)(2,1)}) %all-gather.2.cloned.1.call-update) | async-done | bytes 33554448 | tf_op jit(solution)/shard_map/all_gather | solution.py:31
  156.8 23.7 %fusion.45 = (bf16[512,128,128]{2,1,0:T(8,128)(2,1)}, bf16[512,128,128]{2,1,0:T(8,128)(2,1)}) fusion(bf16[512,256,128]{2,1,0:T(8,128)(2,1)} %all-gather.2.cloned.1.call-done), kind=kLoop, calls=%fused_computation.110 | loop fusion | bytes 67108864 | tf_op jit(solution)/shard_map/slice | solution.py:33
  180.5 158.2 %while.20 = (s32[]{:T(128)}, f32[24,1,8]{0,2,1:T(8,128)S(1)}, f32[24,1,8]{0,2,1:T(8,128)S(1)}, f32[24,1,8,128]{3,0,2,1:T(8,128)S(1)}, s32[512]{0:T(512)S(1)}, /*...) while((s32[]{:T(128)}, f32[24,1,8]{0,2,1:T(8,128)S(1)}, ...), condition=%wide.region_4.5_spmd.clone, body=%wide.region_0.4_spmd.clone.sunk | while | flops 102525072 | bytes 4211027 | solution.py:159
  182.9 1.1 constant_dynamic-slice_fusion.3
  185.4 1.1 constant_dynamic-slice_fusion.3
  187.9 1.1 constant_dynamic-slice_fusion.3
  190.4 1.1 constant_dynamic-slice_fusion.3
  192.8 1.1 constant_dynamic-slice_fusion.3
  195.3 1.1 constant_dynamic-slice_fusion.3
  197.8 1.1 constant_dynamic-slice_fusion.3
  200.2 1.1 constant_dynamic-slice_fusion.3
  202.7 1.1 constant_dynamic-slice_fusion.3
  220.0 1.1 constant_dynamic-slice_fusion.3
  222.5 1.1 constant_dynamic-slice_fusion.3
  225.0 1.1 constant_dynamic-slice_fusion.3
  227.4 1.1 constant_dynamic-slice_fusion.3
  229.9 1.1 constant_dynamic-slice_fusion.3
  232.4 1.1 constant_dynamic-slice_fusion.3
  339.2 5.7 %convolution_bitcast_fusion.1 = f32[4,24,1024]{2,1,0:T(8,128)S(1)} fusion(bf16[24,1024,1]{1,0,2:T(8,128)(2,1)S(1)} %reshape.514, bf16[4,1024,1024]{2,1,0:T(8,128)(2,1)} %bitcast.157), kind=kOutput, calls=%fused_computation.33 | convolution fusion | flops 201326592 | bytes 8830976 | tf_op jit(solution)/shard_map/dot_general | solution.py:192
  344.8 11.4 %all_to_all.10 = f32[4,24,1024]{2,1,0:T(8,128)S(1)} all-to-all(f32[4,24,1024]{2,1,0:T(8,128)S(1)} %convolution_bitcast_fusion.1), channel_id=1, replica_groups=mesh['seq'=64,'tp'=4] {'tp'}, dimensions={0} | all-to-all | bytes 786432 | tf_op jit(solution)/shard_map/all_to_all | solution.py:25
  (820 shorter events, 143.5 us)
Async XLA Ops:
  7.2 2.0 copy-start
  7.2 149.6 %all-gather.2.cloned.1.call-start = ((), (), s32[]{:S(2)}) async-start(), calls=%async_computation.2 | async-start | bytes 34078720 | tf_op jit(solution)/shard_map/all_gather | solution.py:31
  12.6 9.5 %all-to-all-start = ((f32[4,24,256]{2,1,0:T(8,128)}), f32[4,24,256]{2,1,0:T(8,128)S(1)}, u32[]{:S(2)}, u32[]{:S(2)}) async-start(f32[4,24,256]{2,1,0:T(8,128)} %bitcast.133), calls=%async_computation | async-start | bytes 196608 | tf_op jit(solution)/shard_map/all_to_all | solution.py:25
  22.5 39.5 %copy-start.4 = (bf16[3,8,2,128]{3,1,2,0:T(8,128)(2,1)}, bf16[3,8,2,128]{3,1,2,0:T(8,128)(2,1)S(1)}, u32[]{:S(2)}) copy-start(bf16[3,8,2,128]{3,1,2,0:T(8,128)(2,1)S(1)} %copy.60) | copy-start | bytes 36868
  22.5 36.2 %collective-permute-start = (bf16[24,256]{1,0:T(8,128)(2,1)S(1)}, bf16[24,256]{1,0:T(8,128)(2,1)S(1)}, u32[]{:S(2)}, u32[]{:S(2)}) collective-permute-start(bf16[24,256]{1,0:T(8,128)(2,1)S(1)} %bitcast.169), channel_id=1, source_target_pairs={{0,56},{4,60},{8,64},{12,68},{16,72},{20,76},{24,80},{28,84},{32,8... | collective-permute-start | bytes 36872 | tf_op jit(solution)/shard_map/ppermute | solution.py:41
  29.4 34.8 %copy-start.2 = (bf16[24,1024]{1,0:T(8,128)(2,1)S(1)}, bf16[24,1024]{1,0:T(8,128)(2,1)}, u32[]{:S(2)}) copy-start(bf16[24,1024]{1,0:T(8,128)(2,1)} %param.12) | copy-start | bytes 147460
  41.4 20.5 %collective-permute-start.1 = (bf16[24,256]{1,0:T(8,128)(2,1)S(1)}, bf16[24,256]{1,0:T(8,128)(2,1)S(1)}, u32[]{:S(2)}, u32[]{:S(2)}) collective-permute-start(bf16[24,256]{1,0:T(8,128)(2,1)S(1)} %bitcast.170), channel_id=1, source_target_pairs={{0,48},{4,52},{8,56},{12,60},{16,64},{20,68},{24,72},{28,76},{32,8... | collective-permute-start | bytes 36872 | tf_op jit(solution)/shard_map/ppermute | solution.py:41
  46.4 16.9 %collective-permute-start.2 = (bf16[24,256]{1,0:T(8,128)(2,1)S(1)}, bf16[24,256]{1,0:T(8,128)(2,1)S(1)}, u32[]{:S(2)}, u32[]{:S(2)}) collective-permute-start(bf16[24,256]{1,0:T(8,128)(2,1)S(1)} %bitcast.171), channel_id=1, source_target_pairs={{0,40},{4,44},{8,48},{12,52},{16,56},{20,60},{24,64},{28,68},{32,7... | collective-permute-start | bytes 36872 | tf_op jit(solution)/shard_map/ppermute | solution.py:41
  51.6 11.7 %collective-permute-start.3 = (bf16[24,256]{1,0:T(8,128)(2,1)S(1)}, bf16[24,256]{1,0:T(8,128)(2,1)S(1)}, u32[]{:S(2)}, u32[]{:S(2)}) collective-permute-start(bf16[24,256]{1,0:T(8,128)(2,1)S(1)} %bitcast.172), channel_id=1, source_target_pairs={{0,32},{4,36},{8,40},{12,44},{16,48},{20,52},{24,56},{28,60},{32,6... | collective-permute-start | bytes 36872 | tf_op jit(solution)/shard_map/ppermute | solution.py:41
  54.2 9.1 %collective-permute-start.4 = (bf16[24,256]{1,0:T(8,128)(2,1)S(1)}, bf16[24,256]{1,0:T(8,128)(2,1)S(1)}, u32[]{:S(2)}, u32[]{:S(2)}) collective-permute-start(bf16[24,256]{1,0:T(8,128)(2,1)S(1)} %bitcast.173), channel_id=1, source_target_pairs={{0,24},{4,28},{8,32},{12,36},{16,40},{20,44},{24,48},{28,52},{32,5... | collective-permute-start | bytes 36872 | tf_op jit(solution)/shard_map/ppermute | solution.py:41
  58.7 4.6 %collective-permute-start.5 = (bf16[24,256]{1,0:T(8,128)(2,1)S(1)}, bf16[24,256]{1,0:T(8,128)(2,1)S(1)}, u32[]{:S(2)}, u32[]{:S(2)}) collective-permute-start(bf16[24,256]{1,0:T(8,128)(2,1)S(1)} %bitcast.174), channel_id=1, source_target_pairs={{0,16},{4,20},{8,24},{12,28},{16,32},{20,36},{24,40},{28,44},{32,4... | collective-permute-start | bytes 36872 | tf_op jit(solution)/shard_map/ppermute | solution.py:41
  61.9 2.1 collective-permute-start.6
  64.5 115.9 %copy-start.3 = (s32[512]{0:T(512)S(1)}, s32[512]{0:T(512)}, u32[]{:S(2)}) copy-start(s32[512]{0:T(512)} %param.15) | copy-start | bytes 6148
  338.6 18.2 %copy-start.1 = (bf16[24,2048]{1,0:T(8,128)(2,1)S(1)}, bf16[24,2048]{1,0:T(8,128)(2,1)}, u32[]{:S(2)}) copy-start(bf16[24,2048]{1,0:T(8,128)(2,1)} %param.10) | copy-start | bytes 294916
Sparse Core Ops, SparseCore 0:
  10.8 145.9 all-gather.1
where the time goes:
time: 366 us; the launch traced here: 364 us
  local copies, waits for them, and re-layouts  106 us (29%)
  waiting for transfers between devices  95.8 us (26%)
  matrix products  57.5 us (16%)
  other arithmetic  41.2 us (11%)
  starting transfers between devices  32.6 us (9%)
  between operations  14.4 us (4%)
  blocking collectives  11.4 us (3%)
  loops' own time  4.77 us (1%)
    all_gather x1, waiting for transfers between devices, sent_together(): lax.all_gather(both, axis, axis=dim, tiled=True)  92.2 us
    dynamic_slice x64, local copies, waits for them, and re-layouts, one_turn(): lax.dynamic_slice_in_dim(piece_vals, offset_row, turn_pages, 0)  68.4 us
    ppermute x7, starting transfers between devices, passed_along(): return lax.ppermute(array, axis, pairs)  27.7 us
    dot_general x64, matrix products, one_turn(): jnp.einsum('tkgd,pkd->tkgp', query_block, keys_now, preferred_element_typ...  26.3 us
    slice x1, local copies, waits for them, and re-layouts, sent_together(): lax.slice_in_dim(result, at, at + a.shape[along], axis=along)  23.7 us
    dot_general x65, matrix products, online_update(): jnp.einsum('tkgp,pkd->tkgd', weights.astype(jnp.bfloat16), values, prefer...  22.4 us
    reduce_sum x65, other arithmetic, online_update(): totals = totals * factor + jnp.sum(weights, axis=-1)  17.5 us
    dot_general x1, local copies, waits for them, and re-layouts, local(): jnp.dot(attended, out_weight, preferred_element_type=jnp.float32)  12 us
  transfers between devices with their start and end apart: 9, of which 3 were waited for; matrix products, arithmetic and copies ran while one was open for 5% of the time, Pallas kernels for 0%

commit v1 on v0

v1 whole, which is shorter than its diff:
```python
import functools
import math

import jax
import jax.numpy as jnp
import numpy as np
from jax import lax
from jax.experimental import pallas as pl
from jax.experimental.pallas import tpu as pltpu
from jax.sharding import PartitionSpec as P

HD = 128
PAGE = 128
GROUPS = 2
REQS = 8
NY = 4
TP = 4
T = 24
TW = 32
HEADS = 8
PAGES = 8
CHUNK = 4
CK = CHUNK * PAGE
NCH = PAGES // CHUNK
PREFIX = 32768
NEG = -1e30
LOG2E = 1.0 / math.log(2.0)
SCALE2 = LOG2E / math.sqrt(HD)
MSG = HEADS * HD + 128
BF = jnp.bfloat16
F32 = jnp.float32
NT = (((1,), (1,)), ((), ()))
TWO_PI = 2.0 * math.pi


def split_constant(value, bits):
    exponent = math.floor(math.log2(value))
    unit = 2.0 ** (exponent - bits)
    head = math.floor(value / unit) * unit
    return head, value - head


TURN_A, REST = split_constant(TWO_PI, 9)
TURN_B, REST = split_constant(REST, 9)
TURN_C = REST


def lane_iota(shape):
    return lax.broadcasted_iota(jnp.int32, shape, 1)


def row_iota(shape):
    return lax.broadcasted_iota(jnp.int32, shape, 0)


def packed_lse(lse):
    hi = lse.astype(BF).astype(F32)
    rest = lse - hi
    mid = rest.astype(BF).astype(F32)
    low = (rest - mid).astype(BF).astype(F32)
    lane = lane_iota(lse.shape)
    out = jnp.where(lane < 24, pltpu.roll(low, 16, 1), 0.0)
    out = jnp.where(lane < 16, pltpu.roll(mid, 8, 1), out)
    return jnp.where(lane < 8, hi, out).astype(BF)


def unpacked_lse(packed):
    terms = packed.astype(F32)
    return terms + pltpu.roll(terms, 120, 1) + pltpu.roll(terms, 112, 1)


def shares(lses):
    top = functools.reduce(jnp.maximum, lses)
    weights = [jnp.exp2(lse - top) for lse in lses]
    total = functools.reduce(jnp.add, weights)
    inverse = 1.0 / total
    return top, total, [w * inverse for w in weights]


def merged_head(parts, fractions, a):
    out = None
    for part, fraction in zip(parts, fractions):
        f = jnp.broadcast_to(fraction[:, a : a + 1], (T, HD))
        term = part(a) * f
        out = term if out is None else out + term
    return out


def head_of(msg):
    return lambda a: msg[:, a * HD : (a + 1) * HD].astype(F32)


def merge_messages(messages, store):
    lses = [unpacked_lse(m[:, HEADS * HD :]) for m in messages]
    top, total, fractions = shares(lses)
    parts = [head_of(m) for m in messages]
    for a in range(HEADS):
        store[:, a * HD : (a + 1) * HD] = merged_head(parts, fractions, a).astype(BF)
    store[:, HEADS * HD :] = packed_lse(top + jnp.log(total) * LOG2E)


def kernel(
    nz,
    hid_ref,
    kvw_hbm,
    q_ref,
    k_hbm,
    v_hbm,
    pt_ref,
    len_ref,
    freq_ref,
    ow_hbm,
    hidden_ref,
    pages_ref,
    kvw,
    ow,
    kbuf,
    vbuf,
    qbuf,
    qc,
    gmat,
    kp,
    vt,
    acc,
    stat,
    ot,
    st,
    msgs,
    half,
    fromup,
    fromdown,
    sendup,
    senddown,
    kvpart,
    kvin,
    win,
    osuf,
    lsuf,
    att,
    oown,
    osend,
    oin,
    wsem,
    ksend,
    vsend,
    krecv,
    vrecv,
    qsend,
    qrecv,
    q2send,
    q2recv,
    tsend,
    trecv,
    winsend,
    winrecv,
    hsend,
    hrecv,
    upsend,
    uprecv,
    downsend,
    downrecv,
    osendsem,
    orecvsem,
    localsem,
):
    s = lax.axis_index("seq")
    x = lax.axis_index("tp")
    z = s // (2 * NY)
    y = (s // 2) % NY
    c = s % 2
    ups = nz // 2
    downs = nz - 1 - ups

    def seq_at(zz, yy, cc):
        return {"seq": ((zz + nz) % nz * NY + (yy + NY) % NY) * 2 + cc}

    zup, zdown = seq_at(z + 1, y, c), seq_at(z - 1, y, c)
    yup, ydown, yfar = seq_at(z, y + 1, c), seq_at(z, y - 1, c), seq_at(z, y + 2, c)
    other = seq_at(z, y, 1 - c)
    yu, yd, yf = (y + 1) % NY, (y + NY - 1) % NY, (y + 2) % NY

    def remote(src, dst, send, recv, device):
        return pltpu.make_async_remote_copy(
            src_ref=src,
            dst_ref=dst,
            send_sem=send,
            recv_sem=recv,
            device_id=device,
            device_id_type=pl.DeviceIdType.MESH,
        )

    def arrived(ref, sem):
        pltpu.make_async_copy(ref, ref, sem).wait()

    barrier = pltpu.get_barrier_semaphore()
    peers = [zup, zdown, yup, ydown, yfar, other] + [{"tp": (x + i) % TP} for i in range(1, TP)]
    for peer in peers:
        pl.semaphore_signal(barrier, inc=1, device_id=peer, device_id_type=pl.DeviceIdType.MESH)

    own_k = pltpu.make_async_copy(k_hbm, kbuf.at[y], localsem.at[0])
    own_v = pltpu.make_async_copy(v_hbm, vbuf.at[y], localsem.at[1])
    own_q = pltpu.make_async_copy(q_ref, qbuf.at[c, z], localsem.at[2])
    load_kvw = pltpu.make_async_copy(kvw_hbm, kvw, localsem.at[3])
    own_k.start()
    own_v.start()
    own_q.start()
    load_kvw.start()
    load_ow = []
    for i in range(TP):
        target = (x + (2, 1, 3, 0)[i]) % TP
        cols = pl.ds(pl.multiple_of(target * 1024, 1024), 1024)
        load_ow.append(pltpu.make_async_copy(ow_hbm.at[:, cols], ow.at[i], wsem.at[i]))
        load_ow[i].start()
    own_k.wait()
    own_v.wait()
    own_q.wait()
    pl.semaphore_wait(barrier, len(peers))

    sent = []

    def go(copy):
        copy.start()
        sent.append(copy)

    def pass_query(block, step, up):
        device, slot = (zup, step) if up else (zdown, ups + step)
        ref = qbuf.at[c, block]
        go(remote(ref, ref, qsend.at[slot], qrecv.at[block], device))

    def share_query(block):
        ref = qbuf.at[c, block]
        go(remote(ref, ref, q2send.at[block], q2recv.at[block], other))

    pass_query(z, 0, True)
    if downs:
        pass_query(z, 0, False)

    def pages_of(ref, owner, ch):
        return ref.at[owner, pl.ds(ch * CHUNK, CHUNK)]

    for first, second in ((True, False), (False, True)):
        for ch in range(NCH):
            for is_k, device, way in ((first, yup, 0), (second, ydown, 1)):
                buf, ss, rs = (kbuf, ksend, krecv) if is_k else (vbuf, vsend, vrecv)
                ref = pages_of(buf, y, ch)
                go(remote(ref, ref, ss.at[way, ch], rs.at[y, ch], device))
    share_query(z)

    page_row = lax.broadcasted_iota(jnp.int32, (NY * PAGES, 1), 0)
    page_ids = ((z * NY + page_row // PAGES) * 2 + c) * PAGES + page_row % PAGES
    table = pt_ref[...]
    owner = (lane_iota(table.shape) // (table.shape[1] // GROUPS)).astype(F32)
    group_col = jnp.sum(jnp.where(table == page_ids, owner, 0.0), axis=1, keepdims=True)
    gmat[...] = jnp.broadcast_to(group_col, gmat.shape)

    load_kvw.wait()
    for h in range(TP):
        kvpart[h] = jnp.dot(
            hid_ref[...], kvw[:, h * 256 : (h + 1) * 256], preferred_element_type=F32
        )
    for i in (2, 1, 3):
        target = (x + i) % TP
        go(remote(kvpart.at[target], kvin.at[x], tsend.at[i], trecv.at[x], {"tp": target}))

    def query_step(step):
        if step < ups:
            block = (z + nz - 1 - step) % nz
            arrived(qbuf.at[c, block], qrecv.at[block])
            if step + 1 < ups:
                pass_query(block, step + 1, True)
            share_query(block)
        if step < downs:
            block = (z + 1 + step) % nz
            arrived(qbuf.at[c, block], qrecv.at[block])
            if step + 1 < downs:
                pass_query(block, step + 1, False)
            share_query(block)

    query_step(0)

    token = row_iota((T, 1))
    place = (z * NY + y) * T + token
    end = 0
    before = jnp.zeros((T, 1), jnp.int32)
    for r in range(REQS):
        size = len_ref[c, r]
        end = end + size
        before = before + jnp.where(place >= end, size, 0)
    offset = place - before
    position = (PREFIX + offset).astype(F32)
    angle = position * freq_ref[...]
    turns = jnp.floor(angle * (1.0 / TWO_PI) + 0.5)
    reduced = ((angle - turns * TURN_A) - turns * TURN_B) - turns * TURN_C
    cosine = jnp.cos(reduced)
    sine = jnp.sin(reduced)
    sine = jnp.where(lane_iota((T, HD)) < HD // 2, -sine, sine)

    if nz > 2:
        query_step(1)

    total = kvpart[x]
    for i in (1, 3, 2):
        source = (x + i) % TP
        arrived(kvin.at[source], trecv.at[source])
        total = total + kvin[source]
    key, value = total[:, :HD], total[:, HD:]
    rotated = key * cosine + pltpu.roll(key, HD // 2, 1) * sine
    fresh = jnp.concatenate([rotated, value], axis=1)
    pages_ref[...] = fresh.astype(BF)
    win[2, y] = jnp.concatenate([fresh, jnp.zeros((TW - T, 2 * HD), F32)], axis=0).astype(BF)
    mine = win.at[2, y]
    go(remote(mine, mine, winsend.at[0], winrecv.at[y], yup))
    go(remote(mine, mine, winsend.at[1], winrecv.at[y], ydown))
    go(remote(mine, mine, winsend.at[2], winrecv.at[y], yfar))

    for step in range(2, ups):
        query_step(step)

    for source in (yu, yd, yf):
        arrived(win.at[2, source], winrecv.at[source])
    go(remote(win.at[2], win.at[1], winsend.at[3], winrecv.at[NY], zup))

    for i in range(nz):
        arrived(qbuf.at[1 - c, i], q2recv.at[i])
    for zp in range(nz // 2):
        for a in range(HEADS):
            for g in range(GROUPS):
                pair = [
                    qbuf[g, 2 * zp + i, :, a * HD : (a + 1) * HD].astype(F32) for i in range(2)
                ]
                qc[pl.ds(a * nz * T + zp * 2 * T, 2 * T), g * HD : (g + 1) * HD] = (
                    jnp.concatenate(pair, axis=0).astype(BF)
                )

    tiles = HEADS * nz * T // 256
    acc[...] = jnp.zeros_like(acc)
    stat[...] = jnp.where(lax.broadcasted_iota(jnp.int32, stat.shape, 1) < 2, NEG, 0.0)

    def attend(owner_y, ch):
        gates = []
        for j in range(CHUNK):
            page = ch * CHUNK + j
            gate = gmat[pl.ds(owner_y * PAGES + page, 1), :]
            gates.append(gate)
            g1 = gate[:, :HD]
            keys = kbuf[owner_y, page].astype(F32)
            kp[j * PAGE : (j + 1) * PAGE, :] = jnp.concatenate(
                [keys * (1.0 - g1), keys * g1], axis=1
            ).astype(BF)
            vals = vbuf[owner_y, page].astype(F32).T
            vt[:HD, j * PAGE : (j + 1) * PAGE] = (vals * (1.0 - g1)).astype(BF)
            vt[HD:, j * PAGE : (j + 1) * PAGE] = (vals * g1).astype(BF)
        for r in range(tiles):
            scores = lax.dot_general(
                kp[...], qc[r * 256 : (r + 1) * 256, :], NT, preferred_element_type=F32
            )
            parts = [scores[j * PAGE : (j + 1) * PAGE, :] * SCALE2 for j in range(CHUNK)]
            old0, old1 = stat[r, 0:1, :], stat[r, 1:2, :]
            new0, new1 = old0, old1
            for j in range(CHUNK):
                top = jnp.max(parts[j], axis=0, keepdims=True)
                new0 = jnp.maximum(new0, jnp.where(gates[j] > 0.5, NEG, top))
                new1 = jnp.maximum(new1, jnp.where(gates[j] > 0.5, top, NEG))
            fall0, fall1 = jnp.exp2(old0 - new0), jnp.exp2(old1 - new1)
            sum0, sum1 = stat[r, 2:3, :] * fall0, stat[r, 3:4, :] * fall1
            weights = []
            for j in range(CHUNK):
                w = jnp.exp2(parts[j] - jnp.where(gates[j] > 0.5, new1, new0))
                row = jnp.sum(w, axis=0, keepdims=True)
                sum0 = sum0 + jnp.where(gates[j] > 0.5, 0.0, row)
                sum1 = sum1 + jnp.where(gates[j] > 0.5, row, 0.0)
                weights.append(w.astype(BF))
            mixed = jnp.dot(
                vt[...], jnp.concatenate(weights, axis=0), preferred_element_type=F32
            )
            acc[r, :HD, :] = acc[r, :HD, :] * fall0 + mixed[:HD]
            acc[r, HD:, :] = acc[r, HD:, :] * fall1 + mixed[HD:]
            stat[r, 0:1, :] = new0
            stat[r, 1:2, :] = new1
            stat[r, 2:3, :] = sum0
            stat[r, 3:4, :] = sum1

    def forward_pages():
        for ch in range(NCH):
            ref = pages_of(kbuf, yd, ch)
            arrived(ref, krecv.at[yd, ch])
            go(remote(ref, ref, ksend.at[2, ch], krecv.at[yd, ch], yup))
            ref = pages_of(vbuf, yu, ch)
            arrived(ref, vrecv.at[yu, ch])
            go(remote(ref, ref, vsend.at[2, ch], vrecv.at[yu, ch], ydown))

    forward_pages()

    def step(i, carry):
        turn, ch = i // NCH, i % NCH
        owner_y = (y + turn + turn // 2 + (turn // 3) * (NY - 2)) % NY

        @pl.when(turn == 1)
        def _():
            arrived(pages_of(kbuf, yu, ch), krecv.at[yu, ch])

        @pl.when(turn == 2)
        def _():
            arrived(pages_of(vbuf, yd, ch), vrecv.at[yd, ch])

        @pl.when(turn == 3)
        def _():
            arrived(pages_of(kbuf, yf, ch), krecv.at[yf, ch])
            arrived(pages_of(vbuf, yf, ch), vrecv.at[yf, ch])

        attend(owner_y, ch)
        return carry

    def suffix():
        arrived(win.at[1], winrecv.at[NY])
        go(remote(win.at[1], win.at[0], winsend.at[4], winrecv.at[NY + 1], zup))
        arrived(win.at[0], winrecv.at[NY + 1])
        count = 3 * NY * TW
        key_lane = lane_iota((T, count))
        key_z = z - 2 + key_lane // (NY * TW)
        key_place = (key_z * NY + key_lane // TW % NY) * T + key_lane % TW
        seen = (
            (key_lane % TW < T) & (key_place >= 0) & (key_place <= place)
            & (key_place >= place - offset)
        )
        rows = [win[r, b] for r in range(3) for b in range(NY)]
        keys = jnp.concatenate([b[:, :HD] for b in rows], axis=0)
        vals = jnp.concatenate([b[:, HD:] for b in rows], axis=0)
        lse = jnp.zeros((T, HD), F32)
        for a in range(HEADS):
            sc = lax.dot_general(
                q_ref[:, a * HD : (a + 1) * HD], keys, NT, preferred_element_type=F32
            )
            sc = jnp.where(seen, sc * SCALE2, NEG)
            top = jnp.max(sc, axis=1, keepdims=True)
            w = jnp.where(seen, jnp.exp2(sc - top), 0.0)
            tot = jnp.sum(w, axis=1, keepdims=True)
            out = jnp.dot(w.astype(BF), vals, preferred_element_type=F32)
            osuf[:, a * HD : (a + 1) * HD] = out / tot
            lse = jnp.where(lane_iota((T, HD)) == a, top + jnp.log(tot) * LOG2E, lse)
        lsuf[...] = lse

    lax.fori_loop(0, NCH, step, 0)
    suffix()
    lax.fori_loop(NCH, NY * NCH, step, 0)

    for r in range(tiles):
        rows = pl.ds(r * 256, 256)
        s0, s1 = stat[r, 2:3, :], stat[r, 3:4, :]
        ok0, ok1 = s0 > 0.0, s1 > 0.0
        safe0, safe1 = jnp.where(ok0, s0, 1.0), jnp.where(ok1, s1, 1.0)
        inv0, inv1 = 1.0 / safe0, 1.0 / safe1
        lse0 = jnp.where(ok0, stat[r, 0:1, :] + jnp.log(safe0) * LOG2E, NEG)
        lse1 = jnp.where(ok1, stat[r, 1:2, :] + jnp.log(safe1) * LOG2E, NEG)
        ot[rows, :HD] = (acc[r, :HD, :] * inv0).T
        ot[rows, HD:] = (acc[r, HD:, :] * inv1).T
        st[rows, :] = jnp.where(row_iota((HD, 256)) == 0, lse0, lse1).T

    lane = lane_iota((T, HD))

    def build(block, g):
        lse = jnp.zeros((T, HD), F32)
        for a in range(HEADS):
            rows = pl.ds(pl.multiple_of(a * nz * T + block * T, 8), T)
            msgs[g, block, :, a * HD : (a + 1) * HD] = ot[rows, g * HD : (g + 1) * HD].astype(BF)
            col = jnp.broadcast_to(st[rows, g : g + 1], (T, HD))
            lse = jnp.where(lane == a, col, lse)
        msgs[g, block, :, HEADS * HD :] = packed_lse(lse)

    order = []
    for t in range(ups):
        order.append((z + ups - t) % nz)
        if t < downs:
            order.append((z + nz - downs + t) % nz)
    order.append(z)

    for i in range(nz):
        block = order[i]
        for g in range(GROUPS):
            @pl.when(c != g)
            def _():
                build(block, g)
        ref = msgs.at[1 - c, block]
        go(remote(ref, half.at[block], hsend.at[block], hrecv.at[block], other))
    for i in range(nz):
        block = order[i]
        for g in range(GROUPS):
            @pl.when(c == g)
            def _():
                build(block, g)

    def both(block):
        arrived(half.at[block], hrecv.at[block])
        return [msgs[c, block], half[block]]

    for t in range(ups):
        block = (z + ups - t) % nz
        parts = both(block)
        if t:
            arrived(fromup.at[t - 1], uprecv.at[t - 1])
            parts.append(fromup[t - 1])
        merge_messages(parts, sendup.at[t])
        go(remote(sendup.at[t], fromup.at[t], upsend.at[t], uprecv.at[t], zup))
        if t < downs:
            block = (z + nz - downs + t) % nz
            parts = both(block)
            if t:
                arrived(fromdown.at[t - 1], downrecv.at[t - 1])
                parts.append(fromdown[t - 1])
            merge_messages(parts, senddown.at[t])
            go(remote(senddown.at[t], fromdown.at[t], downsend.at[t], downrecv.at[t], zdown))
    last = both(z)
    arrived(fromup.at[ups - 1], uprecv.at[ups - 1])
    last.append(fromup[ups - 1])
    if downs:
        arrived(fromdown.at[downs - 1], downrecv.at[downs - 1])
        last.append(fromdown[downs - 1])
    top, total, fractions = shares(
        [unpacked_lse(m[:, HEADS * HD :]) for m in last] + [lsuf[...]]
    )
    parts = [head_of(m) for m in last] + [lambda a: osuf[:, a * HD : (a + 1) * HD]]
    for a in range(HEADS):
        att[:, a * HD : (a + 1) * HD] = merged_head(parts, fractions, a).astype(BF)

    for i in range(TP):
        load_ow[i].wait()
        partial = jnp.dot(att[...], ow[i], preferred_element_type=F32)
        if i < TP - 1:
            target = (x + (2, 1, 3)[i]) % TP
            osend[i] = partial.astype(BF)
            go(remote(osend.at[i], oin.at[x], osendsem.at[i], orecvsem.at[x], {"tp": target}))
        else:
            oown[...] = partial
    total = oown[...]
    for i in (1, 3, 2):
        source = (x + i) % TP
        arrived(oin.at[source], orecvsem.at[source])
        total = total + oin[source].astype(F32)
    hidden_ref[...] = total.astype(BF)

    for copy in sent:
        copy.wait_send()


def local(
    hidden_in, kv_weight, queries, prefix_keys, prefix_values, page_table, suffix_lengths, out_weight
):
    nz = lax.axis_size("seq") // (2 * NY)
    ups = nz // 2
    downs = max(nz - 1 - ups, 1)
    tiles = HEADS * nz * T // 256
    rows = HEADS * nz * T
    exponent = np.tile(np.arange(HD // 2) * 2.0 / HD, 2)
    freq = (500000.0 ** -exponent).astype(np.float32).reshape(1, HD)
    vmem = pl.BlockSpec(memory_space=pltpu.VMEM)
    anywhere = pl.BlockSpec(memory_space=pl.ANY)
    smem = pl.BlockSpec(memory_space=pltpu.SMEM)
    dma = pltpu.SemaphoreType.DMA
    pages = (NY, PAGES, PAGE, HD)
    scratch = [
        pltpu.VMEM((2048, 1024), BF),
        pltpu.VMEM((TP, 1024, 1024), BF),
        pltpu.VMEM(pages, BF),
        pltpu.VMEM(pages, BF),
        pltpu.VMEM((GROUPS, nz, T, HEADS * HD), BF),
        pltpu.VMEM((rows, GROUPS * HD), BF),
        pltpu.VMEM((NY * PAGES, 256), F32),
        pltpu.VMEM((CK, GROUPS * HD), BF),
        pltpu.VMEM((GROUPS * HD, CK), BF),
        pltpu.VMEM((tiles, GROUPS * HD, 256), F32),
        pltpu.VMEM((tiles, 8, 256), F32),
        pltpu.VMEM((rows, GROUPS * HD), F32),
        pltpu.VMEM((rows, HD), F32),
        pltpu.VMEM((GROUPS, nz, T, MSG), BF),
        pltpu.VMEM((nz, T, MSG), BF),
        pltpu.VMEM((ups, T, MSG), BF),
        pltpu.VMEM((downs, T, MSG), BF),
        pltpu.VMEM((ups, T, MSG), BF),
        pltpu.VMEM((downs, T, MSG), BF),
        pltpu.VMEM((TP, T, 2 * HD), F32),
        pltpu.VMEM((TP, T, 2 * HD), F32),
        pltpu.VMEM((3, NY, TW, 2 * HD), BF),
        pltpu.VMEM((T, HEADS * HD), F32),
        pltpu.VMEM((T, HD), F32),
        pltpu.VMEM((T, HEADS * HD), BF),
        pltpu.VMEM((T, 1024), F32),
        pltpu.VMEM((TP - 1, T, 1024), BF),
        pltpu.VMEM((TP, T, 1024), BF),
        dma((TP,)),
        dma((3, NCH)),
        dma((3, NCH)),
        dma((NY, NCH)),
        dma((NY, NCH)),
        dma((nz,)),
        dma((nz,)),
        dma((nz,)),
        dma((nz,)),
        dma((TP,)),
        dma((TP,)),
        dma((5,)),
        dma((NY + 2,)),
        dma((nz,)),
        dma((nz,)),
        dma((ups,)),
        dma((ups,)),
        dma((downs,)),
        dma((downs,)),
        dma((TP,)),
        dma((TP,)),
        dma((4,)),
    ]
    return pl.pallas_call(
        functools.partial(kernel, nz),
        out_shape=(
            jax.ShapeDtypeStruct((T, 1024), BF),
            jax.ShapeDtypeStruct((T, 2 * HD), BF),
        ),
        in_specs=[vmem, anywhere, vmem, anywhere, anywhere, vmem, smem, vmem, anywhere],
        out_specs=(vmem, vmem),
        scratch_shapes=scratch,
        compiler_params=pltpu.CompilerParams(
            collective_id=0, has_side_effects=True, vmem_limit_bytes=56 * 1024 * 1024
        ),
    )(
        hidden_in,
        kv_weight,
        queries,
        prefix_keys,
        prefix_values,
        page_table.reshape(1, -1),
        suffix_lengths,
        freq,
        out_weight,
    )


def solution(mesh):
    return jax.shard_map(
        local,
        mesh=mesh,
        in_specs=(
            P("seq", "tp"),
            P("tp", None),
            P("seq", "tp"),
            P("seq", None, "tp"),
            P("seq", None, "tp"),
            P(),
            P(),
            P("tp", None),
        ),
        out_specs=(P("seq", "tp"), P("seq", "tp")),
        check_vma=False,
    )
```

time: 366 us -> 72 us (0.20)
  the two profiles are of different devices: /device:TPU:1 before, /device:TPU:2 now
where the time goes in v1:
time: 72 us; the launch traced here: 71.8 us
  Pallas kernels  68.4 us (95%)
  local copies, waits for them, and re-layouts  2.73 us (4%)
    pallas_call x1, Pallas kernels, local(): pl.pallas_call(functools.partial(kernel, nz), out_shape=(jax.ShapeDtypeSt...  68.4 us
    unnamed x2, local copies, waits for them, and re-layouts  2.73 us

profile of v1, /device:TPU:2, one launch (start us, length us, event | category | flops | bytes accessed | tf_op | source)
XLA Modules:
  0.0 71.8 jit_solution(16433030508421158029)
XLA Ops:
  0.6 68.4 %shard_map.104 = (bf16[24,1024]{1,0:T(8,128)(2,1)}, bf16[24,256]{1,0:T(8,128)(2,1)}) custom-call(bf16[24,2048]{1,0:T(8,128)(2,1)} %hid_ref.1, bf16[2048,1024]{1,0:T(8,128)(2,1)} %kvw_hbm.1, bf16[24,1024]{1,0:T(8,128)(2,1)} %q_ref.1, bf16[8,128,128]{2,1,0:T(8,128)(2,1)} %k_hbm.1, bf16[8,128,128]{2,1,0:T(8,128)(2,1)} %v_hbm.1, s32[1,512]{1,0:T(1,128)} %bitcast.1, ...), custom_call_target="tpu_custom_call" | custom-call | tf_op jit(solution)/shard_map/pallas_call | solution.py:612
  69.1 1.4 %copy.13 = bf16[24,1024]{1,0:T(8,128)(2,1)} copy(bf16[24,1024]{1,0:T(8,128)(2,1)} %get-tuple-element.4) | data formatting | bytes 98304
  70.5 1.3 %copy.14 = bf16[24,256]{1,0:T(8,128)(2,1)} copy(bf16[24,256]{1,0:T(8,128)(2,1)} %get-tuple-element.5) | data formatting | bytes 24576

commit v2 on v1

v2 whole, which is shorter than its diff:
```python
import functools
import math

import jax
import jax.numpy as jnp
import numpy as np
from jax import lax
from jax.experimental import pallas as pl
from jax.experimental.pallas import tpu as pltpu
from jax.sharding import PartitionSpec as P

HD = 128
PAGE = 128
GROUPS = 2
REQS = 8
NY = 4
TP = 4
T = 24
TW = 32
HEADS = 8
PAGES = 8
CHUNK = 4
CK = CHUNK * PAGE
NCH = PAGES // CHUNK
PREFIX = 32768
NEG = -1e30
LOG2E = 1.0 / math.log(2.0)
SCALE2 = LOG2E / math.sqrt(HD)
MSG = HEADS * HD + 128
HALVES = ((4, 3, 5, 6), (2, 1, 7, 0))
NEAR_FIRST = (1, 7, 2, 6, 3, 5, 4)
BF = jnp.bfloat16
F32 = jnp.float32
NT = (((1,), (1,)), ((), ()))
TWO_PI = 2.0 * math.pi


def split_constant(value, bits):
    exponent = math.floor(math.log2(value))
    unit = 2.0 ** (exponent - bits)
    head = math.floor(value / unit) * unit
    return head, value - head


TURN_A, REST = split_constant(TWO_PI, 9)
TURN_B, REST = split_constant(REST, 9)
TURN_C = REST


def lane_iota(shape):
    return lax.broadcasted_iota(jnp.int32, shape, 1)


def row_iota(shape):
    return lax.broadcasted_iota(jnp.int32, shape, 0)


def packed_lse(lse):
    hi = lse.astype(BF).astype(F32)
    rest = lse - hi
    mid = rest.astype(BF).astype(F32)
    low = (rest - mid).astype(BF).astype(F32)
    lane = lane_iota(lse.shape)
    out = jnp.where(lane < 24, pltpu.roll(low, 16, 1), 0.0)
    out = jnp.where(lane < 16, pltpu.roll(mid, 8, 1), out)
    return jnp.where(lane < 8, hi, out).astype(BF)


def unpacked_lse(packed):
    terms = packed.astype(F32)
    return terms + pltpu.roll(terms, 120, 1) + pltpu.roll(terms, 112, 1)


def shares(lses):
    top = functools.reduce(jnp.maximum, lses)
    weights = [jnp.exp2(lse - top) for lse in lses]
    total = functools.reduce(jnp.add, weights)
    inverse = 1.0 / total
    return top, total, [w * inverse for w in weights]


def merged_head(parts, fractions, a):
    out = None
    for part, fraction in zip(parts, fractions):
        f = jnp.broadcast_to(fraction[:, a : a + 1], (T, HD))
        term = part(a) * f
        out = term if out is None else out + term
    return out


def head_of(msg):
    return lambda a: msg[:, a * HD : (a + 1) * HD].astype(F32)


def merge_messages(messages, store):
    lses = [unpacked_lse(m[:, HEADS * HD :]) for m in messages]
    top, total, fractions = shares(lses)
    parts = [head_of(m) for m in messages]
    for a in range(HEADS):
        store[:, a * HD : (a + 1) * HD] = merged_head(parts, fractions, a).astype(BF)
    store[:, HEADS * HD :] = packed_lse(top + jnp.log(total) * LOG2E)


def kernel(
    nz,
    hid_ref,
    kvw_hbm,
    q_ref,
    k_hbm,
    v_hbm,
    pt_ref,
    len_ref,
    freq_ref,
    ow_hbm,
    hidden_ref,
    pages_ref,
    kvw,
    ow,
    kbuf,
    vbuf,
    qbuf,
    qc,
    gmat,
    kp,
    vt,
    acc,
    stat,
    ot,
    st,
    msgs,
    half,
    inbox,
    outbox,
    kvpart,
    kvin,
    win,
    osuf,
    lsuf,
    att,
    oown,
    osend,
    oin,
    wsem,
    ksend,
    vsend,
    krecv,
    vrecv,
    qsend,
    qrecv,
    q2send,
    q2recv,
    tsend,
    trecv,
    winsend,
    winrecv,
    hsend,
    hrecv,
    isend,
    irecv,
    osendsem,
    orecvsem,
    localsem,
):
    s = lax.axis_index("seq")
    x = lax.axis_index("tp")
    z = s // (2 * NY)
    y = (s // 2) % NY
    c = s % 2
    def seq_at(zz, yy, cc):
        return {"seq": ((zz + nz) % nz * NY + (yy + NY) % NY) * 2 + cc}

    zup = seq_at(z + 1, y, c)
    yup, ydown, yfar = seq_at(z, y + 1, c), seq_at(z, y - 1, c), seq_at(z, y + 2, c)
    other = seq_at(z, y, 1 - c)
    yu, yd, yf = (y + 1) % NY, (y + NY - 1) % NY, (y + 2) % NY

    def remote(src, dst, send, recv, device):
        return pltpu.make_async_remote_copy(
            src_ref=src,
            dst_ref=dst,
            send_sem=send,
            recv_sem=recv,
            device_id=device,
            device_id_type=pl.DeviceIdType.MESH,
        )

    def arrived(ref, sem):
        pltpu.make_async_copy(ref, ref, sem).wait()

    barrier = pltpu.get_barrier_semaphore()
    peers = [seq_at(z + i, y, c) for i in NEAR_FIRST] + [yup, ydown, yfar, other]
    peers += [{"tp": (x + i) % TP} for i in range(1, TP)]
    for peer in peers:
        pl.semaphore_signal(barrier, inc=1, device_id=peer, device_id_type=pl.DeviceIdType.MESH)

    own_k = pltpu.make_async_copy(k_hbm, kbuf.at[y], localsem.at[0])
    own_v = pltpu.make_async_copy(v_hbm, vbuf.at[y], localsem.at[1])
    own_q = pltpu.make_async_copy(q_ref, qbuf.at[c, z], localsem.at[2])
    load_kvw = pltpu.make_async_copy(kvw_hbm, kvw, localsem.at[3])
    own_k.start()
    own_v.start()
    own_q.start()
    load_kvw.start()
    load_ow = []
    for i in range(TP):
        target = (x + (2, 1, 3, 0)[i]) % TP
        cols = pl.ds(pl.multiple_of(target * 1024, 1024), 1024)
        load_ow.append(pltpu.make_async_copy(ow_hbm.at[:, cols], ow.at[i], wsem.at[i]))
        load_ow[i].start()

    page_row = lax.broadcasted_iota(jnp.int32, (NY * PAGES, 1), 0)
    page_ids = ((z * NY + page_row // PAGES) * 2 + c) * PAGES + page_row % PAGES
    table = pt_ref[...]
    owner = (lane_iota(table.shape) // (table.shape[1] // GROUPS)).astype(F32)
    group_col = jnp.sum(jnp.where(table == page_ids, owner, 0.0), axis=1, keepdims=True)
    gmat[...] = jnp.broadcast_to(group_col, gmat.shape)

    token = row_iota((T, 1))
    place = (z * NY + y) * T + token
    end = 0
    before = jnp.zeros((T, 1), jnp.int32)
    for r in range(REQS):
        size = len_ref[c, r]
        end = end + size
        before = before + jnp.where(place >= end, size, 0)
    offset = place - before
    position = (PREFIX + offset).astype(F32)
    angle = position * freq_ref[...]
    turns = jnp.floor(angle * (1.0 / TWO_PI) + 0.5)
    reduced = ((angle - turns * TURN_A) - turns * TURN_B) - turns * TURN_C
    cosine = jnp.cos(reduced)
    sine = jnp.sin(reduced)
    sine = jnp.where(lane_iota((T, HD)) < HD // 2, -sine, sine)

    load_kvw.wait()
    for h in range(TP):
        kvpart[h] = jnp.dot(
            hid_ref[...], kvw[:, h * 256 : (h + 1) * 256], preferred_element_type=F32
        )

    tiles = HEADS * nz * T // 256
    acc[...] = jnp.zeros_like(acc)
    stat[...] = jnp.where(lax.broadcasted_iota(jnp.int32, stat.shape, 1) < 2, NEG, 0.0)
    own_k.wait()
    own_v.wait()
    own_q.wait()
    pl.semaphore_wait(barrier, len(peers))

    sent = []

    def go(copy):
        copy.start()
        sent.append(copy)

    def share_query(block):
        ref = qbuf.at[c, block]
        go(remote(ref, ref, q2send.at[block], q2recv.at[block], other))

    def query_from(i):
        block = (z + nz - i) % nz
        arrived(qbuf.at[c, block], qrecv.at[block])
        share_query(block)

    mine = qbuf.at[c, z]
    for i in NEAR_FIRST:
        go(remote(mine, mine, qsend.at[i], qrecv.at[z], seq_at(z + i, y, c)))

    def pages_of(ref, owner, ch):
        return ref.at[owner, pl.ds(ch * CHUNK, CHUNK)]

    for first, second in ((True, False), (False, True)):
        for ch in range(NCH):
            for is_k, device, way in ((first, yup, 0), (second, ydown, 1)):
                buf, ss, rs = (kbuf, ksend, krecv) if is_k else (vbuf, vsend, vrecv)
                ref = pages_of(buf, y, ch)
                go(remote(ref, ref, ss.at[way, ch], rs.at[y, ch], device))
    for i in (2, 1, 3):
        target = (x + i) % TP
        go(remote(kvpart.at[target], kvin.at[x], tsend.at[i], trecv.at[x], {"tp": target}))
    share_query(z)
    query_from(1)
    query_from(7)

    total = kvpart[x]
    for i in (1, 3, 2):
        source = (x + i) % TP
        arrived(kvin.at[source], trecv.at[source])
        total = total + kvin[source]
    key, value = total[:, :HD], total[:, HD:]
    rotated = key * cosine + pltpu.roll(key, HD // 2, 1) * sine
    fresh = jnp.concatenate([rotated, value], axis=1)
    pages_ref[...] = fresh.astype(BF)
    win[2, y] = jnp.concatenate([fresh, jnp.zeros((TW - T, 2 * HD), F32)], axis=0).astype(BF)
    mine = win.at[2, y]
    go(remote(mine, mine, winsend.at[0], winrecv.at[y], yup))
    go(remote(mine, mine, winsend.at[1], winrecv.at[y], ydown))
    go(remote(mine, mine, winsend.at[2], winrecv.at[y], yfar))

    def forward_pages(ch):
        for buf, ss, rs, owner_y, device in (
            (kbuf, ksend, krecv, yd, yup),
            (vbuf, vsend, vrecv, yu, ydown),
        ):
            ref = pages_of(buf, owner_y, ch)
            arrived(ref, rs.at[owner_y, ch])
            go(remote(ref, ref, ss.at[2, ch], rs.at[owner_y, ch], device))

    query_from(2)
    query_from(6)
    forward_pages(0)
    query_from(3)
    query_from(5)
    forward_pages(1)

    for source in (yu, yd, yf):
        arrived(win.at[2, source], winrecv.at[source])
    go(remote(win.at[2], win.at[1], winsend.at[3], winrecv.at[NY], zup))
    query_from(4)

    for i in range(nz):
        arrived(qbuf.at[1 - c, i], q2recv.at[i])
    half_rows = HEADS * nz * T // 2
    for h in range(2):
        for p in range(2):
            for a in range(HEADS):
                for g in range(GROUPS):
                    pair = [
                        qbuf[g, (z + HALVES[h][2 * p + i]) % nz, :, a * HD : (a + 1) * HD].astype(F32)
                        for i in range(2)
                    ]
                    qc[pl.ds(h * half_rows + a * 4 * T + p * 2 * T, 2 * T), g * HD : (g + 1) * HD] = (
                        jnp.concatenate(pair, axis=0).astype(BF)
                    )

    def prepare(owner_y, ch, slot):
        for j in range(CHUNK):
            page = ch * CHUNK + j
            gate = gmat[pl.ds(owner_y * PAGES + page, 1), :]
            g1 = gate[:, :HD]
            keys = kbuf[owner_y, page].astype(F32)
            kp[slot, j * PAGE : (j + 1) * PAGE, :] = jnp.concatenate(
                [keys * (1.0 - g1), keys * g1], axis=1
            ).astype(BF)
            vals = vbuf[owner_y, page].astype(F32).T
            vt[slot, :HD, j * PAGE : (j + 1) * PAGE] = (vals * (1.0 - g1)).astype(BF)
            vt[slot, HD:, j * PAGE : (j + 1) * PAGE] = (vals * g1).astype(BF)

    def attend(owner_y, ch, slot, rows):
        first_page = owner_y * PAGES + ch * CHUNK
        gates = [gmat[pl.ds(first_page + j, 1), :] > 0.5 for j in range(CHUNK)]
        for r in rows:
            scores = lax.dot_general(
                kp[slot], qc[r * 256 : (r + 1) * 256, :], NT, preferred_element_type=F32
            )
            parts = [scores[j * PAGE : (j + 1) * PAGE, :] * SCALE2 for j in range(CHUNK)]
            old0, old1 = stat[r, 0:1, :], stat[r, 1:2, :]
            new0, new1 = old0, old1
            for j in range(CHUNK):
                top = jnp.max(parts[j], axis=0, keepdims=True)
                new0 = jnp.maximum(new0, jnp.where(gates[j], NEG, top))
                new1 = jnp.maximum(new1, jnp.where(gates[j], top, NEG))
            fall0, fall1 = jnp.exp2(old0 - new0), jnp.exp2(old1 - new1)
            sum0, sum1 = stat[r, 2:3, :] * fall0, stat[r, 3:4, :] * fall1
            weights = []
            for j in range(CHUNK):
                w = jnp.exp2(parts[j] - jnp.where(gates[j], new1, new0))
                row = jnp.sum(w, axis=0, keepdims=True)
                sum0 = sum0 + jnp.where(gates[j], 0.0, row)
                sum1 = sum1 + jnp.where(gates[j], row, 0.0)
                weights.append(w.astype(BF))
            mixed = jnp.dot(
                vt[slot], jnp.concatenate(weights, axis=0), preferred_element_type=F32
            )
            acc[r, :HD, :] = acc[r, :HD, :] * fall0 + mixed[:HD]
            acc[r, HD:, :] = acc[r, HD:, :] * fall1 + mixed[HD:]
            stat[r, 0:1, :] = new0
            stat[r, 1:2, :] = new1
            stat[r, 2:3, :] = sum0
            stat[r, 3:4, :] = sum1

    def step(i, carry):
        turn, ch = i // NCH, i % NCH
        owner_y = (y + turn + turn // 2) % NY

        @pl.when(turn == 1)
        def _():
            arrived(pages_of(kbuf, yu, ch), krecv.at[yu, ch])

        @pl.when(turn == 2)
        def _():
            arrived(pages_of(vbuf, yd, ch), vrecv.at[yd, ch])

        prepare(owner_y, ch, 0)
        attend(owner_y, ch, 0, range(tiles))
        return carry

    def suffix():
        arrived(win.at[0], winrecv.at[NY + 1])
        count = 3 * NY * TW
        key_lane = lane_iota((T, count))
        key_z = z - 2 + key_lane // (NY * TW)
        key_place = (key_z * NY + key_lane // TW % NY) * T + key_lane % TW
        seen = (
            (key_lane % TW < T) & (key_place >= 0) & (key_place <= place)
            & (key_place >= place - offset)
        )
        rows = [win[r, b] for r in range(3) for b in range(NY)]
        keys = jnp.concatenate([b[:, :HD] for b in rows], axis=0)
        vals = jnp.concatenate([b[:, HD:] for b in rows], axis=0)
        lse = jnp.zeros((T, HD), F32)
        for a in range(HEADS):
            sc = lax.dot_general(
                q_ref[:, a * HD : (a + 1) * HD], keys, NT, preferred_element_type=F32
            )
            sc = jnp.where(seen, sc * SCALE2, NEG)
            top = jnp.max(sc, axis=1, keepdims=True)
            w = jnp.where(seen, jnp.exp2(sc - top), 0.0)
            tot = jnp.sum(w, axis=1, keepdims=True)
            out = jnp.dot(w.astype(BF), vals, preferred_element_type=F32)
            osuf[:, a * HD : (a + 1) * HD] = out / tot
            lse = jnp.where(lane_iota((T, HD)) == a, top + jnp.log(tot) * LOG2E, lse)
        lsuf[...] = lse

    lax.fori_loop(0, NCH, step, 0)
    arrived(win.at[1], winrecv.at[NY])
    go(remote(win.at[1], win.at[0], winsend.at[4], winrecv.at[NY + 1], zup))
    lax.fori_loop(NCH, 3 * NCH, step, 0)

    lane = lane_iota((T, HD))

    def build(h, i, g):
        block = HALVES[h][i]
        lse = jnp.zeros((T, HD), F32)
        for a in range(HEADS):
            rows = pl.ds(h * half_rows + a * 4 * T + i * T, T)
            msgs[g, block, :, a * HD : (a + 1) * HD] = ot[rows, g * HD : (g + 1) * HD].astype(BF)
            col = jnp.broadcast_to(st[rows, g : g + 1], (T, HD))
            lse = jnp.where(lane == a, col, lse)
        msgs[g, block, :, HEADS * HD :] = packed_lse(lse)

    def finish(h):
        for r in range(h * tiles // 2, (h + 1) * tiles // 2):
            rows = pl.ds(r * 256, 256)
            s0, s1 = stat[r, 2:3, :], stat[r, 3:4, :]
            ok0, ok1 = s0 > 0.0, s1 > 0.0
            safe0, safe1 = jnp.where(ok0, s0, 1.0), jnp.where(ok1, s1, 1.0)
            inv0, inv1 = 1.0 / safe0, 1.0 / safe1
            lse0 = jnp.where(ok0, stat[r, 0:1, :] + jnp.log(safe0) * LOG2E, NEG)
            lse1 = jnp.where(ok1, stat[r, 1:2, :] + jnp.log(safe1) * LOG2E, NEG)
            ot[rows, :HD] = (acc[r, :HD, :] * inv0).T
            ot[rows, HD:] = (acc[r, HD:, :] * inv1).T
            st[rows, :] = jnp.where(row_iota((HD, 256)) == 0, lse0, lse1).T
        for i in range(4):
            for g in range(GROUPS):
                build(h, i, g)
        for i in range(4):
            block = HALVES[h][i]
            ref = msgs.at[1 - c, block]
            go(remote(ref, half.at[block], hsend.at[block], hrecv.at[block], other))

    def send_half(h):
        for i in range(4):
            block = HALVES[h][i]
            arrived(half.at[block], hrecv.at[block])
            merge_messages([msgs[c, block], half[block]], outbox.at[block])
            if block:
                go(
                    remote(
                        outbox.at[block],
                        inbox.at[block],
                        isend.at[block],
                        irecv.at[block],
                        seq_at(z + block, y, c),
                    )
                )

    for ch in range(NCH):
        arrived(pages_of(kbuf, yf, ch), krecv.at[yf, ch])
        arrived(pages_of(vbuf, yf, ch), vrecv.at[yf, ch])
        prepare(yf, ch, ch)
    for h in range(2):
        for ch in range(NCH):
            attend(yf, ch, ch, range(h * tiles // 2, (h + 1) * tiles // 2))
        if h:
            send_half(0)
        finish(h)
    send_half(1)
    suffix()

    def gather(blocks, store, narrow):
        messages = [inbox[i] for i in blocks]
        if narrow:
            messages.append(outbox[0])
        lses = [unpacked_lse(m[:, HEADS * HD :]) for m in messages] + [lsuf[...]]
        top, total, fractions = shares(lses)
        parts = [head_of(m) for m in messages]
        parts.append(lambda a: osuf[:, a * HD : (a + 1) * HD])
        for a in range(HEADS):
            out = merged_head(parts, fractions, a)
            store[:, a * HD : (a + 1) * HD] = out.astype(store.dtype)
        if narrow:
            lsuf[...] = top + jnp.log(total) * LOG2E

    for i in NEAR_FIRST[:4]:
        arrived(inbox.at[i], irecv.at[i])
    gather(NEAR_FIRST[:4], osuf, True)
    for i in NEAR_FIRST[4:]:
        arrived(inbox.at[i], irecv.at[i])
    gather(NEAR_FIRST[4:], att, False)

    for i in range(TP):
        load_ow[i].wait()
        partial = jnp.dot(att[...], ow[i], preferred_element_type=F32)
        if i < TP - 1:
            target = (x + (2, 1, 3)[i]) % TP
            osend[i] = partial.astype(BF)
            go(remote(osend.at[i], oin.at[x], osendsem.at[i], orecvsem.at[x], {"tp": target}))
        else:
            oown[...] = partial
    total = oown[...]
    for i in (1, 3, 2):
        source = (x + i) % TP
        arrived(oin.at[source], orecvsem.at[source])
        total = total + oin[source].astype(F32)
    hidden_ref[...] = total.astype(BF)

    for copy in sent:
        copy.wait_send()


def local(
    hidden_in, kv_weight, queries, prefix_keys, prefix_values, page_table, suffix_lengths, out_weight
):
    nz = lax.axis_size("seq") // (2 * NY)
    tiles = HEADS * nz * T // 256
    rows = HEADS * nz * T
    exponent = np.tile(np.arange(HD // 2) * 2.0 / HD, 2)
    freq = (500000.0 ** -exponent).astype(np.float32).reshape(1, HD)
    vmem = pl.BlockSpec(memory_space=pltpu.VMEM)
    anywhere = pl.BlockSpec(memory_space=pl.ANY)
    smem = pl.BlockSpec(memory_space=pltpu.SMEM)
    dma = pltpu.SemaphoreType.DMA
    pages = (NY, PAGES, PAGE, HD)
    scratch = [
        pltpu.VMEM((2048, 1024), BF),
        pltpu.VMEM((TP, 1024, 1024), BF),
        pltpu.VMEM(pages, BF),
        pltpu.VMEM(pages, BF),
        pltpu.VMEM((GROUPS, nz, T, HEADS * HD), BF),
        pltpu.VMEM((rows, GROUPS * HD), BF),
        pltpu.VMEM((NY * PAGES, 256), F32),
        pltpu.VMEM((NCH, CK, GROUPS * HD), BF),
        pltpu.VMEM((NCH, GROUPS * HD, CK), BF),
        pltpu.VMEM((tiles, GROUPS * HD, 256), F32),
        pltpu.VMEM((tiles, 8, 256), F32),
        pltpu.VMEM((rows, GROUPS * HD), F32),
        pltpu.VMEM((rows, HD), F32),
        pltpu.VMEM((GROUPS, nz, T, MSG), BF),
        pltpu.VMEM((nz, T, MSG), BF),
        pltpu.VMEM((nz, T, MSG), BF),
        pltpu.VMEM((nz, T, MSG), BF),
        pltpu.VMEM((TP, T, 2 * HD), F32),
        pltpu.VMEM((TP, T, 2 * HD), F32),
        pltpu.VMEM((3, NY, TW, 2 * HD), BF),
        pltpu.VMEM((T, HEADS * HD), F32),
        pltpu.VMEM((T, HD), F32),
        pltpu.VMEM((T, HEADS * HD), BF),
        pltpu.VMEM((T, 1024), F32),
        pltpu.VMEM((TP - 1, T, 1024), BF),
        pltpu.VMEM((TP, T, 1024), BF),
        dma((TP,)),
        dma((3, NCH)),
        dma((3, NCH)),
        dma((NY, NCH)),
        dma((NY, NCH)),
        dma((nz,)),
        dma((nz,)),
        dma((nz,)),
        dma((nz,)),
        dma((TP,)),
        dma((TP,)),
        dma((5,)),
        dma((NY + 2,)),
        dma((nz,)),
        dma((nz,)),
        dma((nz,)),
        dma((nz,)),
        dma((TP,)),
        dma((TP,)),
        dma((4,)),
    ]
    return pl.pallas_call(
        functools.partial(kernel, nz),
        out_shape=(
            jax.ShapeDtypeStruct((T, 1024), BF),
            jax.ShapeDtypeStruct((T, 2 * HD), BF),
        ),
        in_specs=[vmem, anywhere, vmem, anywhere, anywhere, vmem, smem, vmem, anywhere],
        out_specs=(vmem, vmem),
        scratch_shapes=scratch,
        compiler_params=pltpu.CompilerParams(
            collective_id=0, has_side_effects=True, vmem_limit_bytes=56 * 1024 * 1024
        ),
    )(
        hidden_in,
        kv_weight,
        queries,
        prefix_keys,
        prefix_values,
        page_table.reshape(1, -1),
        suffix_lengths,
        freq,
        out_weight,
    )


def solution(mesh):
    return jax.shard_map(
        local,
        mesh=mesh,
        in_specs=(
            P("seq", "tp"),
            P("tp", None),
            P("seq", "tp"),
            P("seq", None, "tp"),
            P("seq", None, "tp"),
            P(),
            P(),
            P("tp", None),
        ),
        out_specs=(P("seq", "tp"), P("seq", "tp")),
        check_vma=False,
    )
```

time: 72 us -> 69.6 us (0.967)
  the two profiles are of different devices: /device:TPU:2 before, /device:TPU:1 now
where the time goes in v2:
time: 69.6 us; the launch traced here: 69.4 us
  Pallas kernels  66.1 us (95%)
  local copies, waits for them, and re-layouts  2.73 us (4%)
    pallas_call x1, Pallas kernels, local(): pl.pallas_call(functools.partial(kernel, nz), out_shape=(jax.ShapeDtypeSt...  66.1 us
    unnamed x2, local copies, waits for them, and re-layouts  2.73 us

profile of v2, /device:TPU:1, one launch (start us, length us, event | category | flops | bytes accessed | tf_op | source)
XLA Modules:
  0.0 69.4 jit_solution(167395790661322351)
XLA Ops:
  0.6 66.1 %shard_map.104 = (bf16[24,1024]{1,0:T(8,128)(2,1)}, bf16[24,256]{1,0:T(8,128)(2,1)}) custom-call(bf16[24,2048]{1,0:T(8,128)(2,1)} %hid_ref.1, bf16[2048,1024]{1,0:T(8,128)(2,1)} %kvw_hbm.1, bf16[24,1024]{1,0:T(8,128)(2,1)} %q_ref.1, bf16[8,128,128]{2,1,0:T(8,128)(2,1)} %k_hbm.1, bf16[8,128,128]{2,1,0:T(8,128)(2,1)} %v_hbm.1, s32[1,512]{1,0:T(1,128)} %bitcast.1, ...), custom_call_target="tpu_custom_call" | custom-call | tf_op jit(solution)/shard_map/pallas_call | solution.py:592
  66.7 1.4 %copy.13 = bf16[24,1024]{1,0:T(8,128)(2,1)} copy(bf16[24,1024]{1,0:T(8,128)(2,1)} %get-tuple-element.4) | data formatting | bytes 98304
  68.1 1.3 %copy.14 = bf16[24,256]{1,0:T(8,128)(2,1)} copy(bf16[24,256]{1,0:T(8,128)(2,1)} %get-tuple-element.5) | data formatting | bytes 24576
